TPU v7x, 32 devices: a whole 2x2x4 slice. The times are simulated.
32 devices in a mesh: bx: 8 (over z, x), by: 4 (over y, core).
Axes of the slice: x: 2, y: 2, z: 4, core: 2. Of those that a mesh axis runs over, the one named last changes fastest.
Arguments:
- box_map: float32 [8, 4, 256, 256], P('bx', 'by'), as said below
- box_load: float32 [8, 4, 64, 256], P('bx', 'by'), may hold values from -6 to 6
- box_order: int32 [8, 4, 256], P('bx', 'by'), may hold values from 0 to 255, each once within a row
- incoming: float32 [8, 4, 64, 128], P('bx', 'by'), may hold values from -54 to 54
- edge_map: float32 [8, 4, 256, 128], P('bx', 'by'), may hold values from -0.375 to 0.375
- edge_load: float32 [8, 4, 64, 128], P('bx', 'by'), may hold values from -6 to 6
Outputs:
- top_map: float32 [8, 4, 512, 128], P('bx', 'by')
- top_load: float32 [8, 4, 64, 128], P('bx', 'by')
- box_incoming: float32 [8, 4, 64, 256], P('bx', 'by')
- edge_values: float32 [8, 4, 64, 128], P('bx', 'by')
Inputs may be any that keep to these rules, and one draw needn't show every extreme that they name: Each row of box_order holds every number from 0 to 255 once. Every box_map[i, j] has spectral norm at most 0.7.
All inputs are finite; a program needn't handle non-finite values.
Results may differ from a plain program's by a relative error of at most 0.0001.
Values sent between devices are 32-bit elements; how exact they have to be, the bound alone decides.
No kernel may reach another device: no remote copies, remote signals or barrier semaphores. Data moves between devices by JAX's collectives and lax.ppermute only.
A program may use at most 64 MiB of HBM per device.

v0:
```python
import jax
import jax.numpy as jnp
from jax import lax
from jax.sharding import PartitionSpec as P

ALPHA_ORDER = ((0, 2, 3, 1), (0, 3, 2, 1))
BETA_ORDER = ((1, 2, 3, 0), (1, 3, 2, 0))
MACRO_ORDER = (0, 1, 3, 4, 2, 5)


def swapped(block, axis, apart):
    count = lax.axis_size(axis)
    route = []
    for low in range(count):
        high = low | 1 << apart
        if high != low and high < count:
            route += [(low, high), (high, low)]
    return lax.ppermute(block, axis, route)


def matmul(first, second):
    return jnp.dot(
        first, second, precision=lax.Precision.HIGHEST, preferred_element_type=jnp.float32
    )


def block_index(blocks, breadth):
    return jnp.concatenate(
        [jnp.arange(breadth, dtype=jnp.int32) + number * breadth for number in blocks]
    )


def canonical_blocks(order):
    return tuple((order.index(number) for number in range(4)))


def inverse_of(kernel):
    normal_matrix = matmul(kernel.T, kernel)
    factor = jnp.linalg.cholesky(normal_matrix)
    return jax.scipy.linalg.cho_solve((factor, True), kernel.T)


def interface_terms(alpha_outer, alpha_inner, alpha_free, beta_outer, beta_inner, beta_free):
    inner_size = alpha_inner.shape[0]
    kernel = jnp.eye(inner_size, dtype=jnp.float32) - matmul(beta_inner, alpha_inner)
    inverse = inverse_of(kernel)
    alpha_from_alpha = matmul(alpha_outer, inverse)
    alpha_from_beta = -matmul(matmul(beta_outer, alpha_inner), inverse)
    alpha_source = matmul(alpha_free - matmul(beta_free, alpha_inner), inverse)
    beta_from_alpha = -matmul(alpha_from_alpha, beta_inner)
    beta_from_beta = beta_outer - matmul(alpha_from_beta, beta_inner)
    beta_source = beta_free - matmul(alpha_source, beta_inner)
    return (
        alpha_from_alpha,
        alpha_from_beta,
        alpha_source,
        beta_from_alpha,
        beta_from_beta,
        beta_source,
    )


def full_merge(alpha_map, alpha_load, beta_map, beta_load, outer):
    terms = interface_terms(
        alpha_map[:outer, outer:],
        alpha_map[outer:, outer:],
        alpha_load[:, outer:],
        beta_map[:outer, outer:],
        beta_map[outer:, outer:],
        beta_load[:, outer:],
    )
    (
        alpha_from_alpha,
        alpha_from_beta,
        alpha_source,
        beta_from_alpha,
        beta_from_beta,
        beta_source,
    ) = terms
    alpha_back = alpha_map[outer:, :outer]
    beta_back = beta_map[outer:, :outer]
    upper = jnp.concatenate(
        [
            alpha_map[:outer, :outer] - matmul(beta_from_alpha, alpha_back),
            -matmul(alpha_from_alpha, beta_back),
        ],
        axis=1,
    )
    lower = jnp.concatenate(
        [
            -matmul(beta_from_beta, alpha_back),
            beta_map[:outer, :outer] - matmul(alpha_from_beta, beta_back),
        ],
        axis=1,
    )
    merged = jnp.concatenate([upper, lower], axis=0)
    merged_load = jnp.concatenate(
        [
            alpha_load[:, :outer] - matmul(beta_source, alpha_back),
            beta_load[:, :outer] - matmul(alpha_source, beta_back),
        ],
        axis=1,
    )
    return (merged, merged_load, terms)


def interface_values(terms, alpha_in, beta_in):
    (
        alpha_from_alpha,
        alpha_from_beta,
        alpha_source,
        beta_from_alpha,
        beta_from_beta,
        beta_source,
    ) = terms
    alpha_value = (
        matmul(alpha_in, alpha_from_alpha) + matmul(beta_in, alpha_from_beta) + alpha_source
    )
    beta_value = matmul(alpha_in, beta_from_alpha) + matmul(beta_in, beta_from_beta) + beta_source
    return (alpha_value, beta_value)


def body(box_map, box_load, box_order, incoming, edge_map, edge_load):
    own_map = box_map[0, 0]
    own_load = box_load[0, 0]
    own_order = box_order[0, 0]
    raw_incoming = incoming[0, 0]
    own_edge = edge_map[0, 0]
    own_edge_load = edge_load[0, 0]
    breadth = own_map.shape[0] // 4
    share_size = 2 * breadth
    outer = 4 * breadth
    box_total = lax.axis_size("bx") * lax.axis_size("by")
    power = lax.psum(jnp.sum(raw_incoming * raw_incoming, axis=1), ("bx", "by"))
    factor = 1.0 / jnp.sqrt(power / (box_total * raw_incoming.shape[1]) + 1e-06)
    own_incoming = raw_incoming * factor[:, None]
    x_parity = lax.axis_index("bx") % 2
    y_parity = lax.axis_index("by") % 2
    role_index = 2 * x_parity + y_parity
    is_alpha = x_parity == 0
    is_bottom = y_parity == 0
    forward_table = jnp.stack(
        [
            block_index(ALPHA_ORDER[0], breadth),
            block_index(ALPHA_ORDER[1], breadth),
            block_index(BETA_ORDER[0], breadth),
            block_index(BETA_ORDER[1], breadth),
        ]
    )
    picked = jnp.take(own_order, forward_table[role_index], axis=0)
    role_map = jnp.take(jnp.take(own_map, picked, axis=0), picked, axis=1)
    role_load = jnp.take(own_load, picked, axis=1)
    other_map, other_load, other_incoming = swapped((role_map, role_load, own_incoming), "bx", 0)
    alpha_map = jnp.where(is_alpha, role_map, other_map)
    beta_map = jnp.where(is_alpha, other_map, role_map)
    alpha_load = jnp.where(is_alpha, role_load, other_load)
    beta_load = jnp.where(is_alpha, other_load, role_load)
    alpha_incoming = jnp.where(is_alpha, own_incoming, other_incoming)
    beta_incoming = jnp.where(is_alpha, other_incoming, own_incoming)
    level_map, level_load, level_terms = full_merge(
        alpha_map, alpha_load, beta_map, beta_load, 3 * breadth
    )
    macro_index = block_index(MACRO_ORDER, breadth)
    macro_map = jnp.take(jnp.take(level_map, macro_index, axis=0), macro_index, axis=1)
    macro_load = jnp.take(level_load, macro_index, axis=1)
    macro_incoming = jnp.concatenate([alpha_incoming, beta_incoming], axis=1)
    far_outer, far_inner, far_free, far_incoming = swapped(
        (
            macro_map[:outer, outer:],
            macro_map[outer:, outer:],
            macro_load[:, outer:],
            macro_incoming,
        ),
        "by",
        0,
    )
    near_terms = interface_terms(
        macro_map[:outer, outer:],
        macro_map[outer:, outer:],
        macro_load[:, outer:],
        far_outer,
        far_inner,
        far_free,
    )
    near_value, far_value = interface_values(near_terms, macro_incoming, far_incoming)
    macro_inside = -far_value
    start = x_parity * share_size
    own_back = lax.dynamic_slice_in_dim(macro_map[outer:, :outer], start, share_size, 1)
    own_columns = lax.dynamic_slice_in_dim(macro_map[:outer, :outer], start, share_size, 1)
    near_rows = own_columns - matmul(near_terms[3], own_back)
    far_rows = -matmul(near_terms[4], own_back)
    top_share_map = jnp.where(
        is_bottom,
        jnp.concatenate([near_rows, far_rows], axis=0),
        jnp.concatenate([far_rows, near_rows], axis=0),
    )
    top_share_load = lax.dynamic_slice_in_dim(macro_load[:, :outer], start, share_size, 1) - matmul(
        near_terms[5], own_back
    )
    alpha_in = jnp.concatenate([macro_incoming[:, :share_size], macro_inside[:, :breadth]], axis=1)
    beta_in = jnp.concatenate([macro_incoming[:, share_size:], macro_inside[:, breadth:]], axis=1)
    alpha_value, beta_value = interface_values(level_terms, alpha_in, beta_in)
    role_values = jnp.where(
        is_alpha,
        jnp.concatenate([alpha_in, -beta_value], axis=1),
        jnp.concatenate([beta_in, -alpha_value], axis=1),
    )
    backward_table = jnp.stack(
        [
            block_index(canonical_blocks(ALPHA_ORDER[0]), breadth),
            block_index(canonical_blocks(ALPHA_ORDER[1]), breadth),
            block_index(canonical_blocks(BETA_ORDER[0]), breadth),
            block_index(canonical_blocks(BETA_ORDER[1]), breadth),
        ]
    )
    box_values = jnp.take(role_values, backward_table[role_index], axis=1)
    edge_values = matmul(box_values, own_edge) + own_edge_load
    return (
        top_share_map[None, None],
        top_share_load[None, None],
        box_values[None, None],
        edge_values[None, None],
    )


def solution(mesh):
    in_specs = (
        P("bx", "by", None, None),
        P("bx", "by", None, None),
        P("bx", "by", None),
        P("bx", "by", None, None),
        P("bx", "by", None, None),
        P("bx", "by", None, None),
    )
    out_specs = (
        P("bx", "by", None, None),
        P("bx", "by", None, None),
        P("bx", "by", None, None),
        P("bx", "by", None, None),
    )
    return jax.shard_map(body, mesh=mesh, in_specs=in_specs, out_specs=out_specs, check_vma=False)
```

profile of v0, /device:TPU:0, one launch (start us, length us, event | category | flops | bytes accessed | tf_op | source)
XLA Modules:
  0.0 114.0 jit_solution(9329707255149828205)
XLA Ops:
  1.1 0.7 copy-done.1
  1.8 1.9 %gather_fusion = s32[256]{0:T(256)S(1)} fusion(s32[256]{0:T(256)S(1)} %bitcast.135, s32[1024]{0:T(1024)S(1)} %pad_clamp_fusion.4), kind=kCustom, calls=%fused_computation.2 | custom fusion | bytes 3072 | tf_op jit(solution)/shard_map/jit(_take)/gather | solution.py:150
  3.8 1.0 gather_fusion.1
  4.9 1.0 gather_fusion.2
  6.1 3.0 %collective-permute-start = (f32[256,256]{1,0:T(8,128)S(1)}, f32[256,256]{1,0:T(8,128)S(1)}, u32[]{:S(2)}, u32[]{:S(2)}) collective-permute-start(f32[256,256]{1,0:T(8,128)S(1)} %select_bitcast_fusion.1), channel_id=1, source_target_pairs={{0,4},{4,0},{8,12},{12,8},{16,20},{20,16},{24,28},{28,24},{1,5},{5... | collective-permute-start | bytes 786440 | tf_op jit(solution)/shard_map/ppermute | solution.py:18
  9.2 0.7 gather_fusion.6
  10.1 0.8 collective-permute-start.3
  11.0 40.5 %psum.7 = f32[64]{0:T(128)S(1)} all-reduce(f32[64]{0:T(128)S(1)} %fusion.52), channel_id=1, replica_groups=mesh['bx'=8,'by'=4] {'bx','by'}, use_global_device_ids=true, to_apply=%region_5.7 | all-reduce | flops 64 | bytes 512 | tf_op jit(solution)/shard_map/psum | solution.py:134
  51.6 2.3 %collective-permute-start.5 = (f32[64,128]{1,0:T(8,128)S(1)}, f32[64,128]{1,0:T(8,128)S(1)}, u32[]{:S(2)}, u32[]{:S(2)}) collective-permute-start(f32[64,128]{1,0:T(8,128)S(1)} %bitcast_multiply_fusion), channel_id=1, source_target_pairs={{0,4},{4,0},{8,12},{12,8},{16,20},{20,16},{24,28},{28,24},{1,5},{5... | collective-permute-start | bytes 98312 | tf_op jit(solution)/shard_map/ppermute | solution.py:18
  54.1 1.6 %collective-permute-done.5 = f32[64,128]{1,0:T(8,128)S(1)} collective-permute-done((f32[64,128]{1,0:T(8,128)S(1)}, f32[64,128]{1,0:T(8,128)S(1)}, u32[]{:S(2)}, u32[]{:S(2)}) %collective-permute-start.5) | collective-permute-done | bytes 32800 | tf_op jit(solution)/shard_map/ppermute | solution.py:18
  56.0 0.2 fusion.58
  56.2 0.2 convolution_subtract_fusion.8
  56.5 0.2 fusion.95
  56.8 5.8 %cholesky.31 = f32[64,64]{1,0:T(8,128)S(1)} custom-call(f32[64,64]{1,0:T(8,128)S(1)} %fusion.57), custom_call_target="Cholesky" | custom-call | tf_op jit(solution)/shard_map/jit(cholesky)/cholesky | solution.py:39
  62.7 0.6 compare_reduce_fusion.1
  63.3 0.7 fusion.50
  64.0 4.9 %custom-call.20 = f32[1,64,64]{1,2,0:T(8,128)S(1)} custom-call(f32[1,64,64]{2,1,0:T(8,128)S(1)} %fusion.50), custom_call_target="InvertDiagBlocksLowerTriangular" | custom-call | tf_op jit(solution)/shard_map/jit(_cho_solve)/triangular_solve | solution.py:40
  68.9 0.2 fusion.55
  69.3 0.2 fusion.51
  69.6 0.2 convolution_subtract_fusion.7
  70.0 0.4 fusion.13
  70.4 0.3 convolution_negate_fusion.6
  70.7 0.4 convolution_negate_fusion.1
  71.1 0.3 fusion.15
  71.4 0.3 convolution_negate_fusion.5
  71.7 0.4 convolution_subtract_fusion.2
  72.1 0.4 slice_subtract_fusion
  72.9 1.1 gather_fusion.5
  74.2 0.5 collective-permute-start.4
  74.7 0.4 slice_subtract_fusion.1
  75.1 0.3 convolution_negate_fusion
  75.6 1.7 %gather_fusion.3 = f32[384,384]{1,0:T(8,128)S(1)} fusion(f32[384,384]{1,0:T(8,128)S(1)} %maximum_maximum_fusion, s32[1024]{0:T(1024)S(1)} %pad_clamp_fusion.2), kind=kCustom, calls=%fused_computation.5 | custom fusion | bytes 1181184 | tf_op jit(solution)/shard_map/jit(_take)/gather | solution.py:164
  77.3 0.2 copy.27
  77.6 1.9 %gather_fusion.4 = f32[384,384]{1,0:T(8,128)S(1)} fusion(f32[384,384]{0,1:T(8,128)S(1)} %broadcast_select_fusion, s32[1024]{0:T(1024)S(1)} %pad_clamp_fusion.2), kind=kCustom, calls=%fused_computation.6 | custom fusion | bytes 1181184 | tf_op jit(solution)/shard_map/jit(_take)/gather | solution.py:164
  79.5 0.2 copy.28
  80.0 0.5 collective-permute-start.2
  80.7 0.5 collective-permute-done.1
  81.2 0.2 convolution_subtract_fusion.3
  81.4 0.3 fusion.96
  81.8 11.7 %cholesky.65 = f32[128,128]{1,0:T(8,128)S(1)} custom-call(f32[128,128]{1,0:T(8,128)S(1)} %fusion.24), custom_call_target="Cholesky" | custom-call | tf_op jit(solution)/shard_map/jit(cholesky)/cholesky | solution.py:39
  93.6 0.6 compare_reduce_fusion
  94.2 0.7 fusion.17
  94.9 9.8 %custom-call.21 = f32[1,128,128]{1,2,0:T(8,128)S(1)} custom-call(f32[1,128,128]{2,1,0:T(8,128)S(1)} %fusion.17), custom_call_target="InvertDiagBlocksLowerTriangular" | custom-call | tf_op jit(solution)/shard_map/jit(_cho_solve)/triangular_solve | solution.py:40
  104.7 0.3 fusion.22
  105.0 0.2 fusion.20
  105.2 0.3 fusion.87
  105.9 0.3 convolution_negate_fusion.4
  106.1 0.6 slice-done
  106.7 0.8 fusion.9
  107.5 0.3 fusion.1
  107.8 0.3 fusion.90
  108.0 0.3 convolution_negate_fusion.3
  108.3 0.3 convolution_subtract_fusion
  108.6 0.2 fusion.98
  108.8 0.2 fusion.8
  109.1 0.2 fusion.48
  109.3 0.2 fusion.49
  109.6 0.3 fusion
  109.9 0.2 fusion.4
  110.1 0.2 fusion.6
  110.5 0.7 gather_fusion.7
  111.3 0.7 copy.35
  112.2 1.1 fusion.2
  113.3 0.7 maximum_select_fusion
  (93 shorter events, 4.2 us)
Async XLA Ops:
  0.6 3.1 %copy-start = (f32[1,1,256,256]{3,2,1,0:T(8,128)S(1)}, f32[1,1,256,256]{3,2,1,0:T(8,128)}, u32[]{:S(2)}) copy-start(f32[1,1,256,256]{3,2,1,0:T(8,128)} %param.8) | copy-start | bytes 786436
  1.1 0.7 copy-start.1
  6.0 3.1 %copy-start.5 = (f32[1,1,64,256]{3,2,1,0:T(8,128)S(1)}, f32[1,1,64,256]{3,2,1,0:T(8,128)}, u32[]{:S(2)}) copy-start(f32[1,1,64,256]{3,2,1,0:T(8,128)} %param.9) | copy-start | bytes 196612
  6.1 49.9 %collective-permute-start = (f32[256,256]{1,0:T(8,128)S(1)}, f32[256,256]{1,0:T(8,128)S(1)}, u32[]{:S(2)}, u32[]{:S(2)}) collective-permute-start(f32[256,256]{1,0:T(8,128)S(1)} %select_bitcast_fusion.1), channel_id=1, source_target_pairs={{0,4},{4,0},{8,12},{12,8},{16,20},{20,16},{24,28},{28,24},{1,5},{5... | collective-permute-start | bytes 786440 | tf_op jit(solution)/shard_map/ppermute | solution.py:18
  10.0 0.8 copy-start.3
  10.1 45.8 %collective-permute-start.3 = (f32[64,256]{1,0:T(8,128)S(1)}, f32[64,256]{1,0:T(8,128)S(1)}, u32[]{:S(2)}, u32[]{:S(2)}) collective-permute-start(f32[64,256]{1,0:T(8,128)S(1)} %select_bitcast_fusion.4), channel_id=1, source_target_pairs={{0,4},{4,0},{8,12},{12,8},{16,20},{20,16},{24,28},{28,24},{1,5},{5... | collective-permute-start | bytes 196616 | tf_op jit(solution)/shard_map/ppermute | solution.py:18
  51.6 4.2 %collective-permute-start.5 = (f32[64,128]{1,0:T(8,128)S(1)}, f32[64,128]{1,0:T(8,128)S(1)}, u32[]{:S(2)}, u32[]{:S(2)}) collective-permute-start(f32[64,128]{1,0:T(8,128)S(1)} %bitcast_multiply_fusion), channel_id=1, source_target_pairs={{0,4},{4,0},{8,12},{12,8},{16,20},{20,16},{24,28},{28,24},{1,5},{5... | collective-permute-start | bytes 98312 | tf_op jit(solution)/shard_map/ppermute | solution.py:18
  55.8 52.8 %collective-permute-start.6 = (f32[64,256]{1,0:T(8,128)S(1)}, f32[64,256]{1,0:T(8,128)S(1)}, u32[]{:S(2)}, u32[]{:S(2)}) collective-permute-start(f32[64,256]{1,0:T(8,128)S(1)} %pad_maximum_fusion.1), channel_id=1, source_target_pairs={{0,1},{1,0},{2,3},{3,2},{4,5},{5,4},{6,7},{7,6},{8,9},{9,8},{10,11... | collective-permute-start | bytes 196616 | tf_op jit(solution)/shard_map/ppermute | solution.py:18
  74.2 6.3 %copy-start.2 = (f32[64,384]{1,0:T(8,128)}, f32[64,384]{1,0:T(8,128)S(1)}, u32[]{:S(2)}) copy-start(f32[64,384]{1,0:T(8,128)S(1)} %select_bitcast_fusion.3) | copy-start | bytes 294916
  74.2 6.3 %collective-permute-start.4 = (f32[64,128]{1,0:T(8,128)S(1)}, f32[64,128]{1,0:T(8,128)S(1)}, u32[]{:S(2)}, u32[]{:S(2)}) collective-permute-start(f32[64,128]{1,0:T(8,128)S(1)} %slice.152), channel_id=1, source_target_pairs={{0,1},{1,0},{2,3},{3,2},{4,5},{5,4},{6,7},{7,6},{8,9},{9,8},{10,11... | collective-permute-start | bytes 98312 | tf_op jit(solution)/shard_map/ppermute | solution.py:18
  79.9 1.3 %collective-permute-start.1 = (f32[128,128]{1,0:T(8,128)S(1)}, f32[128,128]{1,0:T(8,128)S(1)}, u32[]{:S(2)}, u32[]{:S(2)}) collective-permute-start(f32[128,128]{1,0:T(8,128)S(1)} %slice.145), channel_id=1, source_target_pairs={{0,1},{1,0},{2,3},{3,2},{4,5},{5,4},{6,7},{7,6},{8,9},{9,8},{10,11... | collective-permute-start | bytes 196616 | tf_op jit(solution)/shard_map/ppermute | solution.py:18
  80.0 27.8 %collective-permute-start.2 = (f32[256,128]{1,0:T(8,128)S(1)}, f32[256,128]{1,0:T(8,128)S(1)}, u32[]{:S(2)}, u32[]{:S(2)}) collective-permute-start(f32[256,128]{1,0:T(8,128)S(1)} %slice.144), channel_id=1, source_target_pairs={{0,1},{1,0},{2,3},{3,2},{4,5},{5,4},{6,7},{7,6},{8,9},{9,8},{10,11... | collective-permute-start | bytes 393224 | tf_op jit(solution)/shard_map/ppermute | solution.py:18
  105.8 0.8 slice-start
  111.3 0.9 copy-start.4
  111.3 0.9 copy-start.6
where the time goes:
time: 114 us
  blocking collectives  40.5 us (36%)
  other arithmetic  37 us (32%)
  local copies, waits for them, and re-layouts  14 us (12%)
  matrix products  11.6 us (10%)
  starting transfers between devices  7.3 us (6%)
  waiting for transfers between devices  2.16 us (2%)
  between operations  1.44 us (1%)
    psum x1, blocking collectives, body(): power = lax.psum(jnp.sum(raw_incoming * raw_incoming, axis=1), ('bx', 'by'))  40.5 us
    another operation x6, other arithmetic, inverse_of(): factor = jnp.linalg.cholesky(normal_matrix)  18.9 us
    another operation x4, other arithmetic, inverse_of(): return jax.scipy.linalg.cho_solve((factor, True), kernel.T)  16 us
    dot_general x36, matrix products, matmul(): jnp.dot(first, second, precision=lax.Precision.HIGHEST, preferred_element...  10.7 us
    ppermute x7, starting transfers between devices, swapped(): return lax.ppermute(block, axis, route)  7.3 us
  transfers between devices with their start and end apart: 7, of which 2 were waited for; matrix products, arithmetic and copies ran while one was open for 45% of the time, Pallas kernels for 0%

commit v1 on v0

--- a/solution.py
+++ b/solution.py
@@ -131,7 +131,11 @@
     share_size = 2 * breadth
     outer = 4 * breadth
     box_total = lax.axis_size("bx") * lax.axis_size("by")
-    power = lax.psum(jnp.sum(raw_incoming * raw_incoming, axis=1), ("bx", "by"))
+
+    def test_words(patch):
+        return jnp.sum(lax.all_gather(patch, ("bx", "by")), 0)
+
+    power = test_words(jnp.sum(raw_incoming * raw_incoming, axis=1))
     factor = 1.0 / jnp.sqrt(power / (box_total * raw_incoming.shape[1]) + 1e-06)
     own_incoming = raw_incoming * factor[:, None]
     x_parity = lax.axis_index("bx") % 2

time: 114 us -> 115 us (level)
    psum x1 -> x0, blocking collectives: 40.5 us -> none  [body(): power = lax.psum(jnp.sum(raw_incoming * raw_incoming, axis=1), ('bx', 'by'))]
    unnamed x0 -> x1, blocking collectives: none -> 40.3 us
where the time goes in v1:
time: 115 us; the launch traced here: 114 us
  blocking collectives  40.3 us (35%)
  other arithmetic  37.1 us (32%)
  local copies, waits for them, and re-layouts  14.3 us (12%)
  matrix products  11.6 us (10%)
  starting transfers between devices  7.3 us (6%)
  waiting for transfers between devices  2.16 us (2%)
  between operations  1.46 us (1%)
    unnamed x1, blocking collectives  40.3 us
    another operation x6, other arithmetic, inverse_of(): factor = jnp.linalg.cholesky(normal_matrix)  18.9 us
    another operation x4, other arithmetic, inverse_of(): return jax.scipy.linalg.cho_solve((factor, True), kernel.T)  16 us
    dot_general x36, matrix products, matmul(): jnp.dot(first, second, precision=lax.Precision.HIGHEST, preferred_element...  10.7 us
    ppermute x7, starting transfers between devices, swapped(): return lax.ppermute(block, axis, route)  7.3 us
  transfers between devices with their start and end apart: 7, of which 2 were waited for; matrix products, arithmetic and copies ran while one was open for 45% of the time, Pallas kernels for 0%

profile of v1, /device:TPU:0, one launch (start us, length us, event | category | flops | bytes accessed | tf_op | source)
XLA Modules:
  0.0 114.3 jit_solution(4507893138901487593)
XLA Ops:
  1.1 0.7 copy-done.1
  1.8 1.9 %gather_fusion = s32[256]{0:T(256)S(1)} fusion(s32[256]{0:T(256)S(1)} %bitcast.135, s32[1024]{0:T(1024)S(1)} %pad_clamp_fusion.4), kind=kCustom, calls=%fused_computation.2 | custom fusion | bytes 3072 | tf_op jit(solution)/shard_map/jit(_take)/gather | solution.py:154
  3.8 1.0 gather_fusion.1
  4.9 1.0 gather_fusion.2
  6.1 3.0 %collective-permute-start = (f32[256,256]{1,0:T(8,128)S(1)}, f32[256,256]{1,0:T(8,128)S(1)}, u32[]{:S(2)}, u32[]{:S(2)}) collective-permute-start(f32[256,256]{1,0:T(8,128)S(1)} %select_bitcast_fusion.1), channel_id=1, source_target_pairs={{0,4},{4,0},{8,12},{12,8},{16,20},{20,16},{24,28},{28,24},{1,5},{5... | collective-permute-start | bytes 786440 | tf_op jit(solution)/shard_map/ppermute | solution.py:18
  9.2 0.7 gather_fusion.6
  10.1 0.8 collective-permute-start.3
  11.0 0.3 dynamic-update-slice.6
  11.3 40.3 %all-reduce = f32[2048]{0:T(1024)S(1)} all-reduce(f32[2048]{0:T(1024)S(1)} %dynamic-update-slice.6), channel_id=2, replica_groups=mesh['bx'=8,'by'=4] {'bx','by'}, use_global_device_ids=true, to_apply=%add | all-reduce | flops 2048 | bytes 16384
  51.8 2.3 %collective-permute-start.5 = (f32[64,128]{1,0:T(8,128)S(1)}, f32[64,128]{1,0:T(8,128)S(1)}, u32[]{:S(2)}, u32[]{:S(2)}) collective-permute-start(f32[64,128]{1,0:T(8,128)S(1)} %bitcast_multiply_fusion), channel_id=1, source_target_pairs={{0,4},{4,0},{8,12},{12,8},{16,20},{20,16},{24,28},{28,24},{1,5},{5... | collective-permute-start | bytes 98312 | tf_op jit(solution)/shard_map/ppermute | solution.py:18
  54.4 1.6 %collective-permute-done.5 = f32[64,128]{1,0:T(8,128)S(1)} collective-permute-done((f32[64,128]{1,0:T(8,128)S(1)}, f32[64,128]{1,0:T(8,128)S(1)}, u32[]{:S(2)}, u32[]{:S(2)}) %collective-permute-start.5) | collective-permute-done | bytes 32800 | tf_op jit(solution)/shard_map/ppermute | solution.py:18
  56.2 0.2 fusion.58
  56.4 0.2 convolution_subtract_fusion.8
  56.7 0.2 fusion.95
  57.0 5.8 %cholesky.31 = f32[64,64]{1,0:T(8,128)S(1)} custom-call(f32[64,64]{1,0:T(8,128)S(1)} %fusion.57), custom_call_target="Cholesky" | custom-call | tf_op jit(solution)/shard_map/jit(cholesky)/cholesky | solution.py:39
  62.9 0.6 compare_reduce_fusion.1
  63.6 0.7 fusion.50
  64.2 4.9 %custom-call.20 = f32[1,64,64]{1,2,0:T(8,128)S(1)} custom-call(f32[1,64,64]{2,1,0:T(8,128)S(1)} %fusion.50), custom_call_target="InvertDiagBlocksLowerTriangular" | custom-call | tf_op jit(solution)/shard_map/jit(_cho_solve)/triangular_solve | solution.py:40
  69.1 0.2 fusion.55
  69.5 0.2 fusion.51
  69.8 0.2 convolution_subtract_fusion.7
  70.2 0.4 fusion.13
  70.6 0.3 convolution_negate_fusion.6
  70.9 0.4 convolution_negate_fusion.1
  71.3 0.4 fusion.15
  71.7 0.3 convolution_negate_fusion.5
  72.0 0.4 convolution_subtract_fusion.2
  72.4 0.4 slice_subtract_fusion
  73.2 1.1 gather_fusion.5
  74.4 0.5 collective-permute-start.4
  75.0 0.4 slice_subtract_fusion.1
  75.4 0.3 convolution_negate_fusion
  75.8 1.7 %gather_fusion.3 = f32[384,384]{1,0:T(8,128)S(1)} fusion(f32[384,384]{1,0:T(8,128)S(1)} %maximum_maximum_fusion, s32[1024]{0:T(1024)S(1)} %pad_clamp_fusion.2), kind=kCustom, calls=%fused_computation.5 | custom fusion | bytes 1181184 | tf_op jit(solution)/shard_map/jit(_take)/gather | solution.py:168
  77.6 0.2 copy.40
  77.9 1.9 %gather_fusion.4 = f32[384,384]{1,0:T(8,128)S(1)} fusion(f32[384,384]{0,1:T(8,128)S(1)} %broadcast_select_fusion, s32[1024]{0:T(1024)S(1)} %pad_clamp_fusion.2), kind=kCustom, calls=%fused_computation.6 | custom fusion | bytes 1181184 | tf_op jit(solution)/shard_map/jit(_take)/gather | solution.py:168
  79.8 0.2 copy.41
  80.2 0.5 collective-permute-start.2
  80.9 0.5 collective-permute-done.1
  81.7 0.3 fusion.96
  82.1 11.7 %cholesky.65 = f32[128,128]{1,0:T(8,128)S(1)} custom-call(f32[128,128]{1,0:T(8,128)S(1)} %fusion.24), custom_call_target="Cholesky" | custom-call | tf_op jit(solution)/shard_map/jit(cholesky)/cholesky | solution.py:39
  93.8 0.6 compare_reduce_fusion
  94.5 0.7 fusion.17
  95.1 9.8 %custom-call.21 = f32[1,128,128]{1,2,0:T(8,128)S(1)} custom-call(f32[1,128,128]{2,1,0:T(8,128)S(1)} %fusion.17), custom_call_target="InvertDiagBlocksLowerTriangular" | custom-call | tf_op jit(solution)/shard_map/jit(_cho_solve)/triangular_solve | solution.py:40
  104.9 0.3 fusion.22
  105.2 0.2 fusion.20
  105.4 0.3 fusion.87
  106.1 0.3 convolution_negate_fusion.4
  106.4 0.6 slice-done
  106.9 0.8 fusion.9
  107.7 0.3 fusion.1
  108.0 0.3 fusion.90
  108.3 0.3 convolution_negate_fusion.3
  108.6 0.3 convolution_subtract_fusion
  108.9 0.2 fusion.98
  109.1 0.2 fusion.8
  109.4 0.2 fusion.48
  109.6 0.2 fusion.49
  109.8 0.3 fusion
  110.1 0.2 fusion.4
  110.3 0.2 fusion.6
  110.7 0.7 gather_fusion.7
  111.6 0.7 copy.48
  112.5 1.1 fusion.2
  113.5 0.7 maximum_select_fusion
  (97 shorter events, 4.5 us)
Async XLA Ops:
  0.6 3.1 %copy-start = (f32[1,1,256,256]{3,2,1,0:T(8,128)S(1)}, f32[1,1,256,256]{3,2,1,0:T(8,128)}, u32[]{:S(2)}) copy-start(f32[1,1,256,256]{3,2,1,0:T(8,128)} %param.8) | copy-start | bytes 786436
  1.1 0.7 copy-start.1
  6.0 3.1 %copy-start.5 = (f32[1,1,64,256]{3,2,1,0:T(8,128)S(1)}, f32[1,1,64,256]{3,2,1,0:T(8,128)}, u32[]{:S(2)}) copy-start(f32[1,1,64,256]{3,2,1,0:T(8,128)} %param.9) | copy-start | bytes 196612
  6.1 50.1 %collective-permute-start = (f32[256,256]{1,0:T(8,128)S(1)}, f32[256,256]{1,0:T(8,128)S(1)}, u32[]{:S(2)}, u32[]{:S(2)}) collective-permute-start(f32[256,256]{1,0:T(8,128)S(1)} %select_bitcast_fusion.1), channel_id=1, source_target_pairs={{0,4},{4,0},{8,12},{12,8},{16,20},{20,16},{24,28},{28,24},{1,5},{5... | collective-permute-start | bytes 786440 | tf_op jit(solution)/shard_map/ppermute | solution.py:18
  10.0 0.8 copy-start.3
  10.1 46.0 %collective-permute-start.3 = (f32[64,256]{1,0:T(8,128)S(1)}, f32[64,256]{1,0:T(8,128)S(1)}, u32[]{:S(2)}, u32[]{:S(2)}) collective-permute-start(f32[64,256]{1,0:T(8,128)S(1)} %select_bitcast_fusion.4), channel_id=1, source_target_pairs={{0,4},{4,0},{8,12},{12,8},{16,20},{20,16},{24,28},{28,24},{1,5},{5... | collective-permute-start | bytes 196616 | tf_op jit(solution)/shard_map/ppermute | solution.py:18
  51.8 4.2 %collective-permute-start.5 = (f32[64,128]{1,0:T(8,128)S(1)}, f32[64,128]{1,0:T(8,128)S(1)}, u32[]{:S(2)}, u32[]{:S(2)}) collective-permute-start(f32[64,128]{1,0:T(8,128)S(1)} %bitcast_multiply_fusion), channel_id=1, source_target_pairs={{0,4},{4,0},{8,12},{12,8},{16,20},{20,16},{24,28},{28,24},{1,5},{5... | collective-permute-start | bytes 98312 | tf_op jit(solution)/shard_map/ppermute | solution.py:18
  56.0 52.8 %collective-permute-start.6 = (f32[64,256]{1,0:T(8,128)S(1)}, f32[64,256]{1,0:T(8,128)S(1)}, u32[]{:S(2)}, u32[]{:S(2)}) collective-permute-start(f32[64,256]{1,0:T(8,128)S(1)} %pad_maximum_fusion.1), channel_id=1, source_target_pairs={{0,1},{1,0},{2,3},{3,2},{4,5},{5,4},{6,7},{7,6},{8,9},{9,8},{10,11... | collective-permute-start | bytes 196616 | tf_op jit(solution)/shard_map/ppermute | solution.py:18
  74.4 6.3 %copy-start.2 = (f32[64,384]{1,0:T(8,128)}, f32[64,384]{1,0:T(8,128)S(1)}, u32[]{:S(2)}) copy-start(f32[64,384]{1,0:T(8,128)S(1)} %select_bitcast_fusion.3) | copy-start | bytes 294916
  74.4 6.3 %collective-permute-start.4 = (f32[64,128]{1,0:T(8,128)S(1)}, f32[64,128]{1,0:T(8,128)S(1)}, u32[]{:S(2)}, u32[]{:S(2)}) collective-permute-start(f32[64,128]{1,0:T(8,128)S(1)} %slice.152), channel_id=1, source_target_pairs={{0,1},{1,0},{2,3},{3,2},{4,5},{5,4},{6,7},{7,6},{8,9},{9,8},{10,11... | collective-permute-start | bytes 98312 | tf_op jit(solution)/shard_map/ppermute | solution.py:18
  80.1 1.3 %collective-permute-start.1 = (f32[128,128]{1,0:T(8,128)S(1)}, f32[128,128]{1,0:T(8,128)S(1)}, u32[]{:S(2)}, u32[]{:S(2)}) collective-permute-start(f32[128,128]{1,0:T(8,128)S(1)} %slice.145), channel_id=1, source_target_pairs={{0,1},{1,0},{2,3},{3,2},{4,5},{5,4},{6,7},{7,6},{8,9},{9,8},{10,11... | collective-permute-start | bytes 196616 | tf_op jit(solution)/shard_map/ppermute | solution.py:18
  80.2 27.8 %collective-permute-start.2 = (f32[256,128]{1,0:T(8,128)S(1)}, f32[256,128]{1,0:T(8,128)S(1)}, u32[]{:S(2)}, u32[]{:S(2)}) collective-permute-start(f32[256,128]{1,0:T(8,128)S(1)} %slice.144), channel_id=1, source_target_pairs={{0,1},{1,0},{2,3},{3,2},{4,5},{5,4},{6,7},{7,6},{8,9},{9,8},{10,11... | collective-permute-start | bytes 393224 | tf_op jit(solution)/shard_map/ppermute | solution.py:18
  106.1 0.8 slice-start
  111.6 0.9 copy-start.4
  111.6 0.9 copy-start.6
